TPU v7x, 512 devices: a whole 4x4x16 slice. The times are simulated.
512 devices in a mesh: dp: 64 (over y_lo, z, core), mp: 8 (over y_hi, x).
Axes of the slice: x: 4, y: 4 (y_hi: 2, y_lo: 2; y = y_hi * 2 + y_lo), z: 16, core: 2. Of those that a mesh axis runs over, the one named last changes fastest.
Arguments:
- acts: bfloat16 [16384, 28672], P('dp', 'mp'), may hold values from -24 to 24
- grads: bfloat16 [16384, 8192], P('dp', 'mp'), may hold values from -6 to 6
- basis_in: bfloat16 [28672, 640], P('mp', 'dp'), may hold values from -0.03125 to 0.03125
- basis_out: bfloat16 [8192, 1024], P('dp', 'mp'), may hold values from -0.0625 to 0.0625
- damping: float32 [1], replicated, may hold values from 0.5 to 2
Outputs:
- update: bfloat16 [28672, 8192], P('mp', 'dp')
- diag: float32 [640, 1024], P('mp', 'dp')
All inputs are finite; a program needn't handle non-finite values.
Results may differ from a plain program's by a relative error of at most 0.0085.
Values may be sent and summed in bfloat16 or wider, within the bound.
A program may use at most 64 MiB of HBM per device.

v0:
```python
import jax
import jax.numpy as jnp
from jax import lax
from jax.sharding import PartitionSpec as P


def on_device(acts, grads, basis_in, basis_out, damping):
    tok_rows = acts.shape[0]
    tokens_all = tok_rows * lax.axis_size("dp")
    whole_grads = lax.all_gather(grads, "mp", axis=1, tiled=True)
    grad_proj = jnp.dot(
        whole_grads,
        lax.all_gather(basis_out, "dp", axis=0, tiled=True),
        preferred_element_type=jnp.float32,
    ).astype(jnp.bfloat16)
    full_in = lax.all_gather(basis_in, "dp", axis=1, tiled=True)
    act_proj_t = lax.psum_scatter(
        lax.dot_general(
            full_in, acts, (((0,), (1,)), ((), ())), preferred_element_type=jnp.float32
        ),
        "mp",
        scatter_dimension=0,
        tiled=True,
    ).astype(jnp.bfloat16)
    act_sq_t = (act_proj_t.astype(jnp.float32) ** 2).astype(jnp.bfloat16)
    grad_sq = (grad_proj.astype(jnp.float32) ** 2).astype(jnp.bfloat16)
    stacked = jnp.stack([grad_proj, grad_sq])
    piece = lax.all_gather(stacked, "mp", axis=2, tiled=True)
    rotated = jnp.dot(act_proj_t, piece[0], preferred_element_type=jnp.float32)
    squares = jnp.dot(act_sq_t, piece[1], preferred_element_type=jnp.float32)
    partials = jnp.stack([rotated, squares])
    owned = lax.psum_scatter(partials, "dp", scatter_dimension=2, tiled=True)
    diag = owned[1] / tokens_all
    scaled = (owned[0] / (diag + damping[0])).astype(jnp.bfloat16)
    out_rows = lax.all_gather(basis_out, "mp", axis=1, tiled=True)
    dims = (((1,), (1,)), ((), ()))
    scaled_wide = lax.all_gather(scaled, "dp", axis=1, tiled=True)
    scaled_full = lax.all_gather(scaled_wide, "mp", axis=0, tiled=True)
    back = lax.dot_general(scaled_full, out_rows, dims, preferred_element_type=jnp.float32).astype(
        jnp.bfloat16
    )
    update = jnp.dot(full_in, back, preferred_element_type=jnp.float32)
    return (update.astype(jnp.bfloat16), diag)


def solution(mesh):
    placed = (P("dp", "mp"), P("dp", "mp"), P("mp", "dp"), P("dp", "mp"), P())
    return jax.shard_map(
        on_device,
        mesh=mesh,
        in_specs=placed,
        out_specs=(P("mp", "dp"), P("mp", "dp")),
        check_vma=False,
    )
```

profile of v0, /device:TPU:1, one launch (start us, length us, event | category | flops | bytes accessed | tf_op | source)
XLA Modules:
  0.0 1078.9 jit_solution(1085636390495247304)
XLA Ops:
  7.2 0.7 all-gather.9.cloned.1.call-update
  8.0 0.7 all-gather.7.cloned.1.call-update
  8.7 0.7 all-gather.15.cloned.1.call-update
  9.4 128.3 %all-gather.9.cloned.1.call-done = bf16[8192,128]{1,0:T(8,128)(2,1)} async-done(((bf16[128,128]{1,0:T(8,128)(2,1)}), bf16[8192,128]{1,0:T(8,128)(2,1)}) %all-gather.9.cloned.1.call-update) | async-done | bytes 2097168 | tf_op jit(solution)/shard_map/all_gather | solution.py:13
  137.8 85.6 %all-gather.7.cloned.1.call-done = bf16[256,8192]{1,0:T(8,128)(2,1)} async-done(((bf16[256,1024]{1,0:T(8,128)(2,1)}), bf16[256,8192]{1,0:T(8,128)(2,1)}) %all-gather.7.cloned.1.call-update) | async-done | bytes 4194320 | tf_op jit(solution)/shard_map/all_gather | solution.py:10
  223.4 4.1 convolution_convert_fusion.2
  227.6 0.7 pad_maximum_fusion.1
  228.3 123.6 %all-gather.15.cloned.1.call-done = bf16[64,10,3584]{2,1,0:T(8,128)(2,1)} async-done(((bf16[1,10,3584]{2,1,0:T(8,128)(2,1)}), bf16[64,10,3584]{2,1,0:T(8,128)(2,1)}) %all-gather.15.cloned.1.call-update) | async-done | bytes 4587536 | tf_op jit(solution)/shard_map/all_gather | solution.py:16
  351.9 8.0 reshape.7
  359.9 4.5 fusion.4
  364.5 48.1 %all-gather.11.cloned.1.call-done = bf16[2,256,1024]{2,1,0:T(8,128)(2,1)} async-done(((bf16[2,256,128]{2,1,0:T(8,128)(2,1)}), bf16[2,256,1024]{2,1,0:T(8,128)(2,1)}) %all-gather.11.cloned.1.call-update) | async-done | bytes 1048592 | tf_op jit(solution)/shard_map/all_gather | solution.py:28
  412.5 91.5 %reduce-scatter.2.cloned.1.call-done = f32[80,256]{1,0:T(8,128)} async-done(((f32[640,256]{1,0:T(8,128)}), f32[80,256]{1,0:T(8,128)}) %reduce-scatter.2.cloned.1.call-update) | async-done | bytes 81936 | tf_op jit(solution)/shard_map/reduce_scatter | solution.py:17
  504.0 1.3 convolution_bitcast_fusion
  505.3 1.3 convolution_bitcast_fusion.1
  506.7 1.3 copy.14
  508.8 1.3 dynamic-slice
  510.7 437.4 %all-reduce.3.cloned.1.call-done = f32[2,80,1024]{1,0,2:T(2,128)} async-done(((f32[2,80,1024]{1,0,2:T(2,128)}), f32[2,80,1024]{1,0,2:T(2,128)}) %all-reduce.3.cloned.1.call-update) | async-done | bytes 655376
  948.1 0.8 dynamic-slice_multiply_fusion
  948.9 63.4 %all_gather.25 = bf16[80,1024]{0,1:T(8,128)(2,1)S(1)} all-gather(bf16[80,16]{0,1:T(8,128)(2,1)S(1)} %divide_convert_fusion), channel_id=1, replica_groups=mesh['dp'=64,'mp'=8] {'dp'}, dimensions={1}, use_global_device_ids=true | all-gather | bytes 166400 | tf_op jit(solution)/shard_map/all_gather | solution.py:37
  1012.3 0.8 copy.16
  1013.1 25.8 %all_gather.27 = bf16[128,1024]{1,0:T(8,128)(2,1)S(1)} all-gather(bf16[128,128]{1,0:T(8,128)(2,1)S(1)} %copy-done.1), channel_id=1, replica_groups=mesh['dp'=64,'mp'=8] {'mp'}, dimensions={1}, use_global_device_ids=true | all-gather | bytes 294912 | tf_op jit(solution)/shard_map/all_gather | solution.py:35
  1038.9 27.3 %all-gather.13.cloned.1.call-done = bf16[640,1024]{1,0:T(8,128)(2,1)} async-done(((bf16[80,1024]{1,0:T(8,128)(2,1)}), bf16[640,1024]{1,0:T(8,128)(2,1)}) %all-gather.13.cloned.1.call-update) | async-done | bytes 1310736 | tf_op jit(solution)/shard_map/all_gather | solution.py:38
  1066.1 4.7 fusion
  1070.8 1.3 copy.17
  (20 shorter events, 0.4 us)
Async XLA Ops:
  7.2 352.7 %copy-start = (bf16[256,3584]{1,0:T(8,128)(2,1)S(1)}, bf16[256,3584]{1,0:T(8,128)(2,1)}, u32[]{:S(2)}) copy-start(bf16[256,3584]{1,0:T(8,128)(2,1)} %param.5) | copy-start | bytes 5505028
  7.2 130.6 %all-gather.9.cloned.1.call-start = ((), (), s32[]{:S(2)}) async-start(), calls=%async_computation.3 | async-start | bytes 2129920 | tf_op jit(solution)/shard_map/all_gather | solution.py:13
  7.9 215.5 %all-gather.7.cloned.1.call-start = ((), (), s32[]{:S(2)}) async-start(), calls=%async_computation.2 | async-start | bytes 4718592 | tf_op jit(solution)/shard_map/all_gather | solution.py:10
  8.7 343.2 %all-gather.15.cloned.1.call-start = ((), (), s32[]{:S(2)}) async-start(), calls=%async_computation.6 | async-start | bytes 7454720 | tf_op jit(solution)/shard_map/all_gather | solution.py:16
  9.4 403.1 %all-gather.11.cloned.1.call-start = ((), (), s32[]{:S(2)}) async-start(), calls=%async_computation.4 | async-start | bytes 1179648 | tf_op jit(solution)/shard_map/all_gather | solution.py:28
  228.3 275.8 %reduce-scatter.2.cloned.1.call-start = ((), (), s32[]{:S(2)}) async-start(), calls=%async_computation.1 | async-start | bytes 737280 | tf_op jit(solution)/shard_map/reduce_scatter | solution.py:17
  364.4 583.7 %all-reduce.3.cloned.1.call-start = ((), (), s32[]{:S(2)}) async-start(), calls=%async_computation.7 | async-start | bytes 2097152
  506.7 506.4 %copy-start.1 = (bf16[128,128]{1,0:T(8,128)(2,1)S(1)}, bf16[128,128]{1,0:T(8,128)(2,1)}, u32[]{:S(2)}) copy-start(bf16[128,128]{1,0:T(8,128)(2,1)} %param.8) | copy-start | bytes 98308
  508.1 558.1 %all-gather.13.cloned.1.call-start = ((), (), s32[]{:S(2)}) async-start(), calls=%async_computation.5 | async-start | bytes 1474560 | tf_op jit(solution)/shard_map/all_gather | solution.py:38
  948.9 121.9 %copy-start.2 = (f32[1,80,16]{1,0,2:T(1,128)}, f32[1,80,16]{1,0,2:T(1,128)S(1)}, u32[]{:S(2)}) copy-start(f32[1,80,16]{1,0,2:T(1,128)S(1)} %get-tuple-element.10) | copy-start | bytes 15364
Sparse Core Ops, SparseCore 0:
  10.1 127.6 all-gather.8
  141.0 82.3 all-gather.6
  225.6 126.2 all-gather.14
  354.8 57.7 all-gather.10
  417.4 86.5 reduce-scatter.1
  508.2 439.8 all-reduce.2
  1013.2 52.8 all-gather.12
where the time goes:
time: 1080 us
  waiting for transfers between devices  944 us (87%)
  blocking collectives  89.1 us (8%)
  matrix products  15.9 us (1%)
  between operations  15.5 us (1%)
  local copies, waits for them, and re-layouts  12.7 us (1%)
    unnamed x8, waiting for transfers between devices  440 us
    all_gather x1, waiting for transfers between devices, on_device(): lax.all_gather(basis_out, 'dp', axis=0, tiled=True)  128 us
    all_gather x1, waiting for transfers between devices, on_device(): full_in = lax.all_gather(basis_in, 'dp', axis=1, tiled=True)  124 us
    reduce_scatter x1, waiting for transfers between devices, on_device(): lax.psum_scatter(lax.dot_general(full_in, acts, (((0,), (1,)), ((), ())),...  91.5 us
    all_gather x1, waiting for transfers between devices, on_device(): whole_grads = lax.all_gather(grads, 'mp', axis=1, tiled=True)  85.6 us
    all_gather x1, blocking collectives, on_device(): scaled_wide = lax.all_gather(scaled, 'dp', axis=1, tiled=True)  63.4 us
    all_gather x1, waiting for transfers between devices, on_device(): piece = lax.all_gather(stacked, 'mp', axis=2, tiled=True)  48.1 us
    all_gather x1, waiting for transfers between devices, on_device(): scaled_full = lax.all_gather(scaled_wide, 'mp', axis=0, tiled=True)  27.3 us
  transfers between devices with their start and end apart: 7, of which 7 were waited for; matrix products, arithmetic and copies ran while one was open for 2% of the time, Pallas kernels for 0%

commit v1 on v0

v1 whole, which is shorter than its diff:
```python
import jax
import jax.numpy as jnp
from jax import lax
from jax.experimental import pallas as pl
from jax.experimental.pallas import tpu as pltpu
from jax.sharding import PartitionSpec as P

F32 = jnp.float32
BF16 = jnp.bfloat16
MESH = pl.DeviceIdType.MESH

NZ = 16
NQ = 4
NM = 8
KD = 10
KM = 80
NA = 256
NB = 768
HALF = NA + 2 * NB
LAG = 3


def kernel(
    tokens_all,
    acts, grads, bin_t, bout, damping,
    update, diag_t,
    qa, qb, mix, ga, gb, sb, bo, acc,
    snd_a, snd_g, rcv_a, rcv_g, act, gt, part, r1, p2, r2, sc, bk, bf,
    q_s, q_r, ra_s, ra_r, rb_s, rb_r, yb_s, yb_r, rs_s, rs_r, ys_s, ys_r,
    ca_s, ca_r, cb_s, cb_r, cs_s, cs_r, sw_s, sw_r, bo_s, bo_r,
    xa_s, xa_r, xg_s, xg_r, gt_s, gt_r, p1_s, p1_r, p2_s, p2_r,
    sz_s, sz_r, sq_s, sq_r, bk_s, bk_r,
):
    d = lax.axis_index("dp")
    m = lax.axis_index("mp")
    y = d // 32
    z = (d // 2) % 16
    c = d % 2
    oy = 1 - y
    oc = 1 - c
    me_q = 2 * y + c

    def dev(yy, zz, cc):
        return {"dp": yy * 32 + zz * 2 + cc, "mp": m}

    def copy(src, dst, ssem, rsem, device):
        return pltpu.make_async_remote_copy(
            src_ref=src, dst_ref=dst, send_sem=ssem, recv_sem=rsem,
            device_id=device, device_id_type=MESH,
        )

    here = {"dp": d, "mp": m}
    right = dev(y, (z + 1) % NZ, c)
    left = dev(y, (z + NZ - 1) % NZ, c)
    core = dev(y, z, oc)
    yside = dev(oy, z, c)
    quad = [(y, oc), (oy, c), (oy, oc)]
    swap_a = d // 8
    swap_d = 8 * m + d % 8
    far = swap_a != m

    barrier = pltpu.get_barrier_semaphore()

    def greet(device):
        pl.semaphore_signal(barrier, inc=1, device_id=device, device_id_type=MESH)

    for t in range(1, NZ):
        greet(dev(y, (z + t) % NZ, c))
    for yy, cc in quad:
        greet(dev(yy, z, cc))
    for t in range(1, NM):
        greet({"dp": d, "mp": (m + t) % NM})

    @pl.when(far)
    def _():
        greet({"dp": swap_d, "mp": swap_a})

    a_off = pl.multiple_of(c * HALF, 128)
    b_off = pl.multiple_of(c * HALF + NA + y * NB, 128)
    qa[me_q] = bin_t[:, pl.ds(a_off, NA)]
    qb[me_q] = bin_t[:, pl.ds(b_off, NB)]
    bo[m] = bout[...]

    @pl.when(jnp.logical_not(far))
    def _():
        sb[y, z, c] = bout[...]

    pl.semaphore_wait(barrier, NZ - 1 + 3 + NM - 1 + far.astype(jnp.int32))

    for n, (yy, cc) in enumerate(quad):
        a_to = pl.multiple_of(cc * HALF, 128)
        b_to = pl.multiple_of(cc * HALF + NA + yy * NB, 128)
        copy(bin_t.at[:, pl.ds(a_to, NA)], qa.at[me_q], q_s.at[n, 0], q_r.at[me_q, 0], dev(yy, z, cc)).start()
        copy(bin_t.at[:, pl.ds(b_to, NB)], qb.at[me_q], q_s.at[n, 1], q_r.at[me_q, 1], dev(yy, z, cc)).start()

    @pl.when(far)
    def _():
        copy(bout, sb.at[swap_d // 32, (swap_d // 2) % 16, swap_d % 2], sw_s, sw_r,
             {"dp": swap_d, "mp": swap_a}).start()

    for t in range(1, NM):
        copy(bout, bo.at[m], bo_s.at[t], bo_r.at[m], {"dp": d, "mp": (m + t) % NM}).start()

    for yy, cc in quad:
        s = 2 * yy + cc
        copy(qa.at[s], qa.at[s], q_s.at[0, 0], q_r.at[s, 0], here).wait_recv()
        copy(qb.at[s], qb.at[s], q_s.at[0, 1], q_r.at[s, 1], here).wait_recv()
    for s in range(NQ):
        mix[KD * s:KD * (s + 1), :NA] = qa[s].astype(F32)
        mix[KD * s:KD * (s + 1), NA:] = qb[s].astype(F32)
    ga[c, z] = mix[:40, :NA].astype(BF16)
    gb[c, y, z] = mix[:40, NA:].astype(BF16)

    def ring_a(zz, device):
        copy(ga.at[c, zz], ga.at[c, zz], ra_s, ra_r.at[zz], device).start()

    def ring_b(zz, device):
        copy(gb.at[c, y, zz], gb.at[c, y, zz], rb_s, rb_r.at[zz], device).start()

    def ring_s(yy, zz, device):
        copy(sb.at[yy, zz, c], sb.at[yy, zz, c], rs_s, rs_r.at[yy, zz], device).start()

    def core_a(zz):
        copy(ga.at[c, zz], ga.at[c, zz], ca_s, ca_r, core).start()

    def core_b(yy, zz):
        copy(gb.at[c, yy, zz], gb.at[c, yy, zz], cb_s, cb_r, core).start()

    def core_s(yy, zz):
        copy(sb.at[yy, zz, c], sb.at[yy, zz, c], cs_s, cs_r, core).start()

    def y_b(zz):
        copy(gb.at[c, y, zz], gb.at[c, y, zz], yb_s, yb_r.at[zz], yside).start()

    def got_a(zz):
        copy(ga.at[c, zz], ga.at[c, zz], ra_s, ra_r.at[zz], here).wait_recv()

    def got_b(zz):
        copy(gb.at[c, y, zz], gb.at[c, y, zz], rb_s, rb_r.at[zz], here).wait_recv()

    def got_s(yy, zz):
        copy(sb.at[yy, zz, c], sb.at[yy, zz, c], rs_s, rs_r.at[yy, zz], here).wait_recv()

    def got_y(zz):
        copy(gb.at[c, oy, zz], gb.at[c, oy, zz], yb_s, yb_r.at[zz], here).wait_recv()
        core_b(oy, zz)

    ring_b(z, right)
    ring_b(z, left)
    ring_a(z, right)
    ring_a(z, left)
    y_b(z)
    core_b(y, z)
    core_a(z)

    def step(s, _):
        zr = (z - s + NZ) % NZ
        zl = (z + s) % NZ

        @pl.when(s <= 8)
        def _():
            got_b(zr)

            @pl.when(s < 8)
            def _():
                ring_b(zr, right)

            y_b(zr)
            core_b(y, zr)

            @pl.when(s < 8)
            def _():
                got_b(zl)

                @pl.when(s < 7)
                def _():
                    ring_b(zl, left)

                y_b(zl)
                core_b(y, zl)

            got_a(zr)

            @pl.when(s < 8)
            def _():
                ring_a(zr, right)

            core_a(zr)

            @pl.when(s < 8)
            def _():
                got_a(zl)

                @pl.when(s < 7)
                def _():
                    ring_a(zl, left)

                core_a(zl)

        @pl.when(s == LAG)
        def _():
            @pl.when(far)
            def _():
                copy(sb.at[y, z, c], sb.at[y, z, c], sw_s, sw_r, here).wait_recv()

            copy(sb.at[y, z, c], sb.at[y, z, c], ys_s, ys_r, yside).start()
            ring_s(y, z, right)
            ring_s(y, z, left)
            core_s(y, z)
            copy(sb.at[oy, z, c], sb.at[oy, z, c], ys_s, ys_r, here).wait_recv()
            ring_s(oy, z, right)
            ring_s(oy, z, left)
            core_s(oy, z)

        @pl.when(s > LAG)
        def _():
            t = s - LAG
            sr = (z - t + NZ) % NZ
            sl = (z + t) % NZ
            for yy in (y, oy):
                got_s(yy, sr)

                @pl.when(t < 8)
                def _():
                    ring_s(yy, sr, right)

                core_s(yy, sr)

                @pl.when(t < 8)
                def _():
                    got_s(yy, sl)

                    @pl.when(t < 7)
                    def _():
                        ring_s(yy, sl, left)

                    core_s(yy, sl)

        @pl.when(s <= 9)
        def _():
            t = s - 1
            got_y((z - t + NZ) % NZ)

            @pl.when((t > 0) & (t < 8))
            def _():
                got_y((z + t) % NZ)

        return 0

    lax.fori_loop(1, 9 + LAG, step, 0)

    copy(ga.at[oc], ga.at[oc], ca_s, ca_r, here).wait_recv()
    copy(gb.at[oc], gb.at[oc], cb_s, cb_r, here).wait_recv()

    first = True
    for cc in range(2):
        for off, piece, width in (
            (cc * HALF, ga.at[cc], NA),
            (cc * HALF + NA, gb.at[cc, 0], NB),
            (cc * HALF + NA + NB, gb.at[cc, 1], NB),
        ):
            for k in range(0, width, 256):
                lhs = piece[:, :, k:k + 256].reshape(NZ * 40, 256)
                prod = lax.dot_general(
                    lhs, acts[:, off + k:off + k + 256], (((1,), (1,)), ((), ())),
                    preferred_element_type=F32,
                )
                if first:
                    acc[...] = prod
                    first = False
                else:
                    acc[...] += prod
    for mm in range(NM):
        yy, z0 = mm // 4, 4 * (mm % 4)
        for i in range(4):
            src = 40 * (z0 + i) + 20 * yy
            mix[20 * i:20 * (i + 1), :256] = acc[src:src + 20, :]
        snd_a[mm] = mix[:KM, :256].astype(BF16)
    for t in range(1, NM):
        to = (m + t) % NM
        copy(snd_a.at[to], rcv_a.at[m], xa_s.at[t], xa_r.at[m], {"dp": d, "mp": to}).start()
    rcv_a[m] = snd_a[m]

    copy(sb.at[:, :, oc], sb.at[:, :, oc], cs_s, cs_r, here).wait_recv()
    for mm in range(NM):
        yy, z0 = mm // 4, 4 * (mm % 4)
        block = sb[yy, z0:z0 + 4].reshape(1024, 128)
        snd_g[mm] = jnp.dot(grads[...], block, preferred_element_type=F32).astype(BF16)
    for t in range(1, NM):
        to = (m + t) % NM
        copy(snd_g.at[to], rcv_g.at[m], xg_s.at[t], xg_r.at[m], {"dp": d, "mp": to}).start()
    rcv_g[m] = snd_g[m]

    for t in range(1, NM):
        s = (m + t) % NM
        copy(rcv_a.at[s], rcv_a.at[s], xa_s.at[t], xa_r.at[s], here).wait_recv()
    total = rcv_a[0].astype(F32)
    for s in range(1, NM):
        total += rcv_a[s].astype(F32)
    act[...] = jnp.zeros_like(act)
    act[:KM, :] = total.astype(BF16)

    for t in range(1, NM):
        s = (m + t) % NM
        copy(rcv_g.at[s], rcv_g.at[s], xg_s.at[t], xg_r.at[s], here).wait_recv()
    total = rcv_g[0].astype(F32)
    for s in range(1, NM):
        total += rcv_g[s].astype(F32)
    gt[m] = total.T.astype(BF16)
    for t in range(1, NM):
        to = (m + t) % NM
        copy(gt.at[m], gt.at[m], gt_s.at[t], gt_r.at[m], {"dp": d, "mp": to}).start()
    for t in range(1, NM):
        s = (m + t) % NM
        copy(gt.at[s], gt.at[s], gt_s.at[t], gt_r.at[s], here).wait_recv()

    nt = (((1,), (1,)), ((), ()))
    a_val = act[...]
    a_sq = (a_val.astype(F32) ** 2).astype(BF16)
    for mm in range(NM):
        yy, z0 = mm // 4, 4 * (mm % 4)
        g_val = gt[mm]
        g_sq = (g_val.astype(F32) ** 2).astype(BF16)
        rot = lax.dot_general(g_val, a_val, nt, preferred_element_type=F32).astype(BF16)
        sq = lax.dot_general(g_sq, a_sq, nt, preferred_element_type=F32).astype(BF16)
        for i in range(8):
            part[yy, z0 + i // 2, i % 2, 0] = rot[16 * i:16 * (i + 1), :]
            part[yy, z0 + i // 2, i % 2, 1] = sq[16 * i:16 * (i + 1), :]
    for n, (yy, cc) in enumerate(quad):
        copy(part.at[yy, :, cc], r1.at[me_q], p1_s.at[n], p1_r.at[me_q], dev(yy, z, cc)).start()
    r1[me_q] = part[y, :, c]
    for yy, cc in quad:
        s = 2 * yy + cc
        copy(r1.at[s], r1.at[s], p1_s.at[0], p1_r.at[s], here).wait_recv()
    total = r1[0].astype(F32)
    for s in range(1, NQ):
        total += r1[s].astype(F32)
    p2[...] = total.astype(BF16)
    for t in range(1, NZ):
        to = (z + t) % NZ
        copy(p2.at[to], r2.at[z], p2_s.at[t], p2_r.at[z], dev(y, to, c)).start()
    r2[z] = p2[z]
    for t in range(1, NZ):
        s = (z + t) % NZ
        copy(r2.at[s], r2.at[s], p2_s.at[t], p2_r.at[s], here).wait_recv()
    total = r2[0].astype(F32)
    for s in range(1, NZ):
        total += r2[s].astype(F32)
    diag = total[1] / tokens_all
    diag_t[...] = diag[:, :KM]
    sc[y, z, c] = (total[0] / (diag + damping[0])).astype(BF16)

    for t in range(1, NZ):
        copy(sc.at[y, z, c], sc.at[y, z, c], sz_s.at[t], sz_r.at[z], dev(y, (z + t) % NZ, c)).start()
    for t in range(1, NZ):
        s = (z + t) % NZ
        copy(sc.at[y, s, c], sc.at[y, s, c], sz_s.at[t], sz_r.at[s], here).wait_recv()
    for n, (yy, cc) in enumerate(quad):
        copy(sc.at[y, :, c], sc.at[y, :, c], sq_s.at[n], sq_r.at[me_q], dev(yy, z, cc)).start()
    for yy, cc in quad:
        copy(sc.at[yy, :, cc], sc.at[yy, :, cc], sq_s.at[0], sq_r.at[2 * yy + cc], here).wait_recv()
    for t in range(1, NM):
        s = (m + t) % NM
        copy(bo.at[s], bo.at[s], bo_s.at[t], bo_r.at[s], here).wait_recv()

    total = jnp.zeros((128, 128), F32)
    for mm in range(NM):
        yy, z0 = mm // 4, 4 * (mm % 4)
        total += jnp.dot(bo[mm], sc[yy, z0:z0 + 4].reshape(128, 128), preferred_element_type=F32)
    bk[m] = total.T[:KM, :].astype(BF16)
    for t in range(1, NM):
        copy(bk.at[m], bk.at[m], bk_s.at[t], bk_r.at[m], {"dp": d, "mp": (m + t) % NM}).start()
    for t in range(1, NM):
        s = (m + t) % NM
        copy(bk.at[s], bk.at[s], bk_s.at[t], bk_r.at[s], here).wait_recv()
    for mm in range(NM):
        yy, z0 = mm // 4, 4 * (mm % 4)
        b_val = bk[mm].astype(F32)
        for i in range(4):
            dst = 40 * (z0 + i) + 20 * yy
            bf[dst:dst + 20, :] = b_val[20 * i:20 * (i + 1), :]
    back_t = bf[...].T.astype(BF16)
    for cc in range(2):
        for off, piece, width in (
            (cc * HALF, ga.at[cc], NA),
            (cc * HALF + NA, gb.at[cc, 0], NB),
            (cc * HALF + NA + NB, gb.at[cc, 1], NB),
        ):
            for k in range(0, width, 256):
                rhs = piece[:, :, k:k + 256].reshape(NZ * 40, 256)
                up = jnp.dot(back_t, rhs, preferred_element_type=F32)
                update[off + k:off + k + 256, :] = up.T.astype(BF16)

    for n in range(3):
        copy(qa.at[0], qa.at[0], q_s.at[n, 0], q_r.at[0, 0], here).wait_send()
        copy(qb.at[0], qb.at[0], q_s.at[n, 1], q_r.at[0, 0], here).wait_send()
        copy(r1.at[0], r1.at[0], p1_s.at[n], p1_r.at[0], here).wait_send()
        copy(sc.at[y, :, c], sc.at[y, :, c], sq_s.at[n], sq_r.at[0], here).wait_send()

    @pl.when(far)
    def _():
        copy(bout, bout, sw_s, sw_r, here).wait_send()

    for t in range(1, NM):
        copy(bout, bout, bo_s.at[t], bo_r.at[0], here).wait_send()
        copy(snd_a.at[0], snd_a.at[0], xa_s.at[t], xa_r.at[0], here).wait_send()
        copy(snd_g.at[0], snd_g.at[0], xg_s.at[t], xg_r.at[0], here).wait_send()
        copy(gt.at[0], gt.at[0], gt_s.at[t], gt_r.at[0], here).wait_send()
        copy(bk.at[0], bk.at[0], bk_s.at[t], bk_r.at[0], here).wait_send()
    for t in range(1, NZ):
        copy(p2.at[0], p2.at[0], p2_s.at[t], p2_r.at[0], here).wait_send()
        copy(sc.at[0, 0, 0], sc.at[0, 0, 0], sz_s.at[t], sz_r.at[0], here).wait_send()
    copy(ga.at[0, pl.ds(0, 15)], ga.at[0, pl.ds(0, 15)], ra_s, ra_r.at[0], here).wait_send()
    copy(gb.at[0, 0, pl.ds(0, 15)], gb.at[0, 0, pl.ds(0, 15)], rb_s, rb_r.at[0], here).wait_send()
    copy(gb.at[0, 0], gb.at[0, 0], yb_s, yb_r.at[0], here).wait_send()
    copy(sb.at[:, pl.ds(0, 15), 0], sb.at[:, pl.ds(0, 15), 0], rs_s, rs_r.at[0, 0], here).wait_send()
    copy(sb.at[0, 0, 0], sb.at[0, 0, 0], ys_s, ys_r, here).wait_send()
    copy(ga.at[0], ga.at[0], ca_s, ca_r, here).wait_send()
    copy(gb.at[0], gb.at[0], cb_s, cb_r, here).wait_send()
    copy(sb.at[:, :, 0], sb.at[:, :, 0], cs_s, cs_r, here).wait_send()


def solution(mesh):
    def on_device(acts, grads, basis_in, basis_out, damping):
        tokens_all = acts.shape[0] * mesh.shape["dp"]
        vmem = pl.BlockSpec(memory_space=pltpu.VMEM)
        dma = pltpu.SemaphoreType.DMA
        v = pltpu.VMEM

        def body(*refs):
            kernel(tokens_all, *refs)

        update, diag_t = pl.pallas_call(
            body,
            out_shape=(
                jax.ShapeDtypeStruct((3584, 128), BF16),
                jax.ShapeDtypeStruct((16, KM), F32),
            ),
            in_specs=[vmem] * 4 + [pl.BlockSpec(memory_space=pltpu.SMEM)],
            out_specs=(vmem, vmem),
            scratch_shapes=[
                v((NQ, KD, NA), BF16), v((NQ, KD, NB), BF16), v((KM, NA + NB), F32),
                v((2, NZ, 40, NA), BF16), v((2, 2, NZ, 40, NB), BF16),
                v((2, NZ, 2, 128, 128), BF16), v((NM, 128, 128), BF16), v((640, 256), F32),
                v((NM, KM, 256), BF16), v((NM, 256, 128), BF16),
                v((NM, KM, 256), BF16), v((NM, 256, 128), BF16),
                v((128, 256), BF16), v((NM, 128, 256), BF16),
                v((2, NZ, 2, 2, 16, 128), BF16), v((NQ, NZ, 2, 16, 128), BF16),
                v((NZ, 2, 16, 128), BF16), v((NZ, 2, 16, 128), BF16),
                v((2, NZ, 2, 16, 128), BF16), v((NM, KM, 128), BF16), v((640, 128), F32),
                dma((3, 2)), dma((NQ, 2)), dma, dma((NZ,)), dma, dma((NZ,)), dma, dma((NZ,)),
                dma, dma((2, NZ)), dma, dma,
                dma, dma, dma, dma, dma, dma, dma, dma, dma((NM,)), dma((NM,)),
                dma((NM,)), dma((NM,)), dma((NM,)), dma((NM,)), dma((NM,)), dma((NM,)),
                dma((3,)), dma((NQ,)), dma((NZ,)), dma((NZ,)),
                dma((NZ,)), dma((NZ,)), dma((3,)), dma((NQ,)), dma((NM,)), dma((NM,)),
            ],
            compiler_params=pltpu.CompilerParams(
                collective_id=0, has_side_effects=True, vmem_limit_bytes=48 * 2**20
            ),
        )(acts, grads, basis_in.T, basis_out, damping)
        return update, diag_t.T

    placed = (P("dp", "mp"), P("dp", "mp"), P("mp", "dp"), P("dp", "mp"), P())
    return jax.shard_map(
        on_device,
        mesh=mesh,
        in_specs=placed,
        out_specs=(P("mp", "dp"), P("mp", "dp")),
        check_vma=False,
    )
```

time: 1080 us -> 132 us (0.12)
  waiting for transfers between devices: 944 us -> 0 us
  Pallas kernels: 0 us -> 125 us
  blocking collectives: 89.1 us -> 0 us
  matrix products: 15.9 us -> 0 us
  between operations: 15.5 us -> 1.3 us
    unnamed x8 -> x0, waiting for transfers between devices: 440 us -> none
    all_gather x5 -> x0, waiting for transfers between devices: 413 us -> none  [the longest x1 128 us: on_device(): lax.all_gather(basis_out, 'dp', axis=0, tiled=True)]
    pallas_call x0 -> x1, Pallas kernels: none -> 125 us  [on_device(): pl.pallas_call(body, out_shape=(jax.ShapeDtypeStruct((3584, 128), BF16),...]
    reduce_scatter x1 -> x0, waiting for transfers between devices: 91.5 us -> none  [on_device(): lax.psum_scatter(lax.dot_general(full_in, acts, (((0,), (1,)), ((), ())),...]
    all_gather x2 -> x0, blocking collectives: 89.1 us -> none  [the longest x1 63.4 us: on_device(): scaled_wide = lax.all_gather(scaled, 'dp', axis=1, tiled=True)]
    dot_general x5 -> x0, matrix products: 15.9 us -> none  [the longest x1 4.67 us: on_device(): update = jnp.dot(full_in, back, preferred_element_type=jnp.float32)]
  transfers between devices with their start and end apart: 7 -> 0, of which waited for: 7 -> 0; matrix products, arithmetic and copies ran while one was open for 2% -> 0% of each run, Pallas kernels for 0% -> 0%
where the time goes in v1:
time: 132 us
  Pallas kernels  125 us (95%)
  local copies, waits for them, and re-layouts  5.71 us (4%)
    pallas_call x1, Pallas kernels, on_device(): pl.pallas_call(body, out_shape=(jax.ShapeDtypeStruct((3584, 128), BF16),...  125 us
    unnamed x10, local copies, waits for them, and re-layouts  5.71 us

profile of v1, /device:TPU:1, one launch (start us, length us, event | category | flops | bytes accessed | tf_op | source)
XLA Modules:
  0.0 131.6 jit_solution(15004438333482086121)
XLA Ops:
  1.3 0.0 copy-start
  1.3 1.5 %copy-done = bf16[256,3584]{1,0:T(8,128)(2,1)S(1)} copy-done((bf16[256,3584]{1,0:T(8,128)(2,1)S(1)}, bf16[256,3584]{1,0:T(8,128)(2,1)}, u32[]{:S(2)}) %copy-start) | copy-done | bytes 1835032
  2.8 0.0 copy-start.1
  2.8 1.0 copy-done.1
  3.8 0.0 copy-start.2
  3.8 0.9 copy-done.2
  4.7 0.0 copy-start.3
  4.7 0.8 copy-done.3
  5.5 124.6 %shard_map.68 = (bf16[3584,128]{1,0:T(8,128)(2,1)S(1)}, f32[16,80]{1,0:T(8,128)S(1)}) custom-call(bf16[256,3584]{1,0:T(8,128)(2,1)S(1)} %copy-done, bf16[256,1024]{1,0:T(8,128)(2,1)S(1)} %copy-done.1, bf16[10,3584]{1,0:T(8,128)(2,1)S(1)} %bitcast.2, bf16[128,128]{1,0:T(8,128)(2,1)S(1)} %copy-done.3, f32[1]{0:T(128)S(6)} %copy.9.refs_4_), custom_call_target="tpu_custom_call" | custom-call | tf_op jit(solution)/shard_map/pallas_call | solution.py:433
  130.1 0.9 copy.10
  131.0 0.6 copy.11
Async XLA Ops:
  1.3 1.5 %copy-start = (bf16[256,3584]{1,0:T(8,128)(2,1)S(1)}, bf16[256,3584]{1,0:T(8,128)(2,1)}, u32[]{:S(2)}) copy-start(bf16[256,3584]{1,0:T(8,128)(2,1)} %refs_0_.1) | copy-start | bytes 5505028
  2.8 1.0 copy-start.1
  3.8 0.9 copy-start.2
  4.7 0.8 copy-start.3

commit v2 on v0

v2 whole, which is shorter than its diff:
```python
import jax
import jax.numpy as jnp
from jax import lax
from jax.experimental import pallas as pl
from jax.experimental.pallas import tpu as pltpu
from jax.sharding import PartitionSpec as P

F32 = jnp.float32
BF16 = jnp.bfloat16
MESH = pl.DeviceIdType.MESH

NZ = 16
NQ = 4
NM = 8
KD = 10
KM = 80
NA = 1024
NB = 384
HALF = NA + 2 * NB
SLAG = 1
NC = 4
YLAG = 2


def kernel(
    tokens_all,
    acts_h, grads_h, bin_t, bout, damping,
    update, diag_t,
    acts, grads,
    qa, qb, mix, ga, gb, sb, bo, acc,
    snd_a, snd_g, rcv_a, rcv_g, act, own_g, gt, part, r1, p2, r2, sc, bk, bf,
    q_s, q_r, ra_s, ra_r, rb_s, rb_r, yb_s, yb_r, rs_s, rs_r, ys_s, ys_r,
    ca_s, ca_r, cb_s, cb_r, cs_s, cs_r, sw_s, sw_r, bo_s, bo_r,
    xa_s, xa_r, xg_s, xg_r, gt_s, gt_r, p1_s, p1_r, p2_s, p2_r,
    sz_s, sz_r, sq_s, sq_r, bk_s, bk_r, in_s, ac_s, ac_r,
):
    d = lax.axis_index("dp")
    m = lax.axis_index("mp")
    y = d // 32
    z = (d // 2) % 16
    c = d % 2
    oy = 1 - y
    oc = 1 - c
    me_q = 2 * y + c
    d_other = d + 1 - 2 * c

    def dev(yy, zz, cc):
        return {"dp": yy * 32 + zz * 2 + cc, "mp": m}

    def copy(src, dst, ssem, rsem, device):
        return pltpu.make_async_remote_copy(
            src_ref=src, dst_ref=dst, send_sem=ssem, recv_sem=rsem,
            device_id=device, device_id_type=MESH,
        )

    here = {"dp": d, "mp": m}
    right = dev(y, (z + 1) % NZ, c)
    left = dev(y, (z + NZ - 1) % NZ, c)
    core = dev(y, z, oc)
    yside = dev(oy, z, c)
    quad = [(y, oc), (oy, c), (oy, oc)]
    swap_a = d // 8
    swap_d = 8 * m + d % 8
    far = swap_a != m

    act[:, KM:, :] = jnp.zeros((2, 128 - KM, 256), BF16)
    barrier = pltpu.get_barrier_semaphore()

    def greet(device):
        pl.semaphore_signal(barrier, inc=1, device_id=device, device_id_type=MESH)

    for t in range(1, NZ):
        greet(dev(y, (z + t) % NZ, c))
    for yy, cc in quad:
        greet(dev(yy, z, cc))
    for t in range(1, NM):
        greet({"dp": d, "mp": (m + t) % NM})
        greet({"dp": d_other, "mp": (m + t) % NM})

    @pl.when(far)
    def _():
        greet({"dp": swap_d, "mp": swap_a})

    a_off = pl.multiple_of(c * HALF, 128)
    b_off = pl.multiple_of(c * HALF + NA + y * NB, 128)
    own_a = pltpu.make_async_copy(bin_t.at[:, pl.ds(a_off, NA)], qa.at[me_q], in_s.at[0])
    own_b = pltpu.make_async_copy(bin_t.at[:, pl.ds(b_off, NB)], qb.at[me_q], in_s.at[1])
    own_o = pltpu.make_async_copy(bout, bo.at[m], in_s.at[2])
    own_s = pltpu.make_async_copy(bout, sb.at[y, z, c], in_s.at[3])
    get_g = pltpu.make_async_copy(grads_h, grads, in_s.at[4])
    get_a = pltpu.make_async_copy(acts_h, acts, in_s.at[5])
    own_a.start()
    own_b.start()
    own_o.start()

    @pl.when(jnp.logical_not(far))
    def _():
        own_s.start()

    get_g.start()
    get_a.start()
    pl.semaphore_wait(barrier, NZ - 1 + 3 + 2 * (NM - 1) + far.astype(jnp.int32))

    @pl.when(far)
    def _():
        copy(bout, sb.at[swap_d // 32, (swap_d // 2) % 16, swap_d % 2], sw_s, sw_r,
             {"dp": swap_d, "mp": swap_a}).start()

    for yy, cc in quad:
        a_to = pl.multiple_of(cc * HALF, 128)
        b_to = pl.multiple_of(cc * HALF + NA + yy * NB, 128)
        copy(bin_t.at[:, pl.ds(a_to, NA)], qa.at[me_q], q_s.at[0], q_r.at[0], dev(yy, z, cc)).start()
        copy(bin_t.at[:, pl.ds(b_to, NB)], qb.at[me_q], q_s.at[1], q_r.at[1], dev(yy, z, cc)).start()
    for t in range(1, NM):
        copy(bout, bo.at[m], bo_s, bo_r, {"dp": d, "mp": (m + t) % NM}).start()

    def ring_a(q):
        def send(zz, device):
            copy(ga.at[c, q, zz], ga.at[c, q, zz], ra_s, ra_r.at[q, zz], device).start()

        return send

    def ring_b(zz, device):
        copy(gb.at[c, y, zz], gb.at[c, y, zz], rb_s, rb_r.at[zz], device).start()

    def ring_s(zz, device):
        copy(sb.at[y, zz, c], sb.at[y, zz, c], rs_s, rs_r.at[zz], device).start()

    def side_b(zz):
        copy(gb.at[c, y, zz], gb.at[c, y, zz], yb_s, yb_r.at[zz], yside).start()
        core_b(y, zz)

    def side_s(zz):
        copy(sb.at[y, zz, c], sb.at[y, zz, c], ys_s, ys_r.at[zz], yside).start()
        core_s(y, zz)

    def core_a(q):
        def send(zz):
            copy(ga.at[c, q, zz], ga.at[c, q, zz], ca_s, ca_r, core).start()

        return send

    def core_b(yy, zz):
        copy(gb.at[c, yy, zz], gb.at[c, yy, zz], cb_s, cb_r, core).start()

    def core_s(yy, zz):
        copy(sb.at[yy, zz, c], sb.at[yy, zz, c], cs_s, cs_r.at[yy], core).start()

    def got_a(q):
        def wait(zz):
            copy(ga.at[c, q, zz], ga.at[c, q, zz], ra_s, ra_r.at[q, zz], here).wait_recv()

        return wait

    def got_b(zz):
        copy(gb.at[c, y, zz], gb.at[c, y, zz], rb_s, rb_r.at[zz], here).wait_recv()

    def got_s(zz):
        copy(sb.at[y, zz, c], sb.at[y, zz, c], rs_s, rs_r.at[zz], here).wait_recv()

    def got_yb(zz):
        copy(gb.at[c, oy, zz], gb.at[c, oy, zz], yb_s, yb_r.at[zz], here).wait_recv()
        core_b(oy, zz)

    def got_ys(zz):
        copy(sb.at[oy, zz, c], sb.at[oy, zz, c], ys_s, ys_r.at[zz], here).wait_recv()
        core_s(oy, zz)

    own_a.wait()
    own_b.wait()
    copy(qa.at[:3], qa.at[:3], q_s.at[0], q_r.at[0], here).wait_recv()
    copy(qb.at[:3], qb.at[:3], q_s.at[1], q_r.at[1], here).wait_recv()
    for s in range(NQ):
        mix[KD * s:KD * (s + 1), :NA] = qa[s].astype(F32)
        mix[KD * s:KD * (s + 1), NA:] = qb[s].astype(F32)
    for q in range(NC):
        ga[c, q, z] = mix[:40, 256 * q:256 * (q + 1)].astype(BF16)
    gb[c, y, z] = mix[:40, NA:].astype(BF16)

    for q in range(NC):
        ring_a(q)(z, right)
        ring_a(q)(z, left)
        core_a(q)(z)
    ring_b(z, right)
    ring_b(z, left)
    side_b(z)

    def hop(t, got, ring, side):
        zr = (z - t + NZ) % NZ
        zl = (z + t) % NZ
        got(zr)

        @pl.when(t < 8)
        def _():
            ring(zr, right)

        side(zr)

        @pl.when(t < 8)
        def _():
            got(zl)

            @pl.when(t < 7)
            def _():
                ring(zl, left)

            side(zl)

    def side_hop(t, got):
        got((z - t + NZ) % NZ)

        @pl.when((t > 0) & (t < 8))
        def _():
            got((z + t) % NZ)

    def step(s, _):
        @pl.when(s <= 8)
        def _():
            for q in range(NC):
                hop(s, got_a(q), ring_a(q), core_a(q))
            hop(s, got_b, ring_b, side_b)

        @pl.when(s == SLAG)
        def _():
            @pl.when(far)
            def _():
                copy(sb.at[y, z, c], sb.at[y, z, c], sw_s, sw_r, here).wait_recv()

            @pl.when(jnp.logical_not(far))
            def _():
                own_s.wait()

            ring_s(z, right)
            ring_s(z, left)
            side_s(z)

        @pl.when((s > SLAG) & (s <= SLAG + 8))
        def _():
            hop(s - SLAG, got_s, ring_s, side_s)

        @pl.when((s >= YLAG) & (s <= YLAG + 8))
        def _():
            side_hop(s - YLAG, got_yb)

        @pl.when(s >= SLAG + YLAG)
        def _():
            side_hop(s - SLAG - YLAG, got_ys)

        return 0

    def grad_part(col):
        copy(sb.at[col, :, oc], sb.at[col, :, oc], cs_s, cs_r.at[col], here).wait_recv()
        for k in (2, 1, 3, 0):
            z0 = (m % 4 + k) % 4
            to = 4 * col + z0
            block = sb[col, pl.ds(4 * z0, 4)].reshape(1024, 128)
            snd_g[to] = jnp.dot(grads[...], block, preferred_element_type=F32).astype(BF16)

            @pl.when(to != m)
            def _():
                copy(snd_g.at[to], rcv_g.at[m], xg_s, xg_r, {"dp": d, "mp": to}).start()

            @pl.when(to == m)
            def _():
                rcv_g[m] = snd_g[to]

    def act_part(off, piece, width):
        lhs = piece[...].reshape(NZ * 40, width)
        return lax.dot_general(
            lhs, acts[:, off:off + width], (((1,), (1,)), ((), ())), preferred_element_type=F32
        )

    def act_first():
        get_a.wait()
        copy(ga.at[oc], ga.at[oc], ca_s, ca_r, here).wait_recv()
        acc[...] = act_part(0, ga.at[0, 0], 256)
        for cc in range(2):
            for q in range(NC):
                if cc or q:
                    acc[...] += act_part(cc * HALF + 256 * q, ga.at[cc, q], 256)

    def act_rest():
        copy(gb.at[oc], gb.at[oc], cb_s, cb_r, here).wait_recv()
        for cc in range(2):
            for yy in range(2):
                acc[...] += act_part(cc * HALF + NA + yy * NB, gb.at[cc, yy], NB)
        for mm in range(NM):
            yy, z0 = mm // 4, 4 * (mm % 4)
            for i in range(4):
                src = 40 * (z0 + i) + 20 * yy
                mix[20 * i:20 * (i + 1), :256] = acc[src:src + 20, :]
            snd_a[mm] = mix[:KM, :256].astype(BF16)
        for t in range(1, NM):
            to = (m + t) % NM
            copy(snd_a.at[to], rcv_a.at[m], xa_s, xa_r, {"dp": d, "mp": to}).start()
        rcv_a[m] = snd_a[m]


    lax.fori_loop(1, 9, step, 0)
    act_first()
    lax.fori_loop(9, 9 + SLAG, step, 0)
    get_g.wait()
    grad_part(y)
    lax.fori_loop(9 + SLAG, 9 + YLAG, step, 0)
    act_rest()
    lax.fori_loop(9 + YLAG, 9 + SLAG + YLAG, step, 0)
    grad_part(oy)

    copy(rcv_g.at[:7], rcv_g.at[:7], xg_s, xg_r, here).wait_recv()
    total = rcv_g[0].astype(F32)
    for s in range(1, NM):
        total += rcv_g[s].astype(F32)
    g_t = total.T.astype(BF16)
    for i in range(8):
        own_g[i % 2, 16 * (i // 2):16 * (i // 2 + 1), :] = g_t[16 * i:16 * (i + 1), :]
    mine_g = c * NM + m
    for t in range(1, NM):
        to = (m + t) % NM
        copy(own_g.at[c], gt.at[mine_g], gt_s, gt_r, {"dp": d, "mp": to}).start()
        copy(own_g.at[oc], gt.at[mine_g], gt_s, gt_r, {"dp": d_other, "mp": to}).start()
    copy(own_g.at[oc], gt.at[mine_g], gt_s, gt_r, core).start()
    gt[mine_g] = own_g[c]
    copy(rcv_a.at[:7], rcv_a.at[:7], xa_s, xa_r, here).wait_recv()
    total = rcv_a[0].astype(F32)
    for s in range(1, NM):
        total += rcv_a[s].astype(F32)
    act[c, :KM, :] = total.astype(BF16)
    copy(act.at[c, :KM], act.at[c, :KM], ac_s, ac_r, core).start()
    copy(act.at[oc, :KM], act.at[oc, :KM], ac_s, ac_r, here).wait_recv()

    copy(gt.at[:15], gt.at[:15], gt_s, gt_r, here).wait_recv()

    nt = (((1,), (1,)), ((), ()))
    groups = [(z // 4 + q) % 4 for q in (2, 1, 3, 0)]
    for half in (oy, y):
        rot = jnp.zeros((256, 128), F32)
        sq = jnp.zeros((256, 128), F32)
        for cc in range(2):
            a_val = act[cc]
            g_val = gt[pl.ds(cc * NM + 4 * half, 4)].reshape(256, 256)
            rot += lax.dot_general(g_val, a_val, nt, preferred_element_type=F32)
            a_sq = (a_val.astype(F32) ** 2).astype(BF16)
            g_sq = (g_val.astype(F32) ** 2).astype(BF16)
            sq += lax.dot_general(g_sq, a_sq, nt, preferred_element_type=F32)
        part[half, :, 0] = rot.astype(BF16).reshape(NZ, 16, 128)
        part[half, :, 1] = sq.astype(BF16).reshape(NZ, 16, 128)
        if half is oy:
            for q, g in enumerate(groups):
                mine = pl.ds(4 * g, 4)
                copy(part.at[oy, mine], r1.at[mine], p1_s, p1_r.at[q], yside).start()
    for q, g in enumerate(groups):
        mine = pl.ds(4 * g, 4)
        copy(r1.at[:4], r1.at[:4], p1_s, p1_r.at[q], here).wait_recv()
        p2[mine] = (part[y, mine].astype(F32) + r1[mine].astype(F32)).astype(BF16)
        for i in range(4):
            to = 4 * g + i

            @pl.when(to != z)
            def _():
                copy(p2.at[to], r2.at[z], p2_s, p2_r, dev(y, to, c)).start()
    r2[z] = p2[z]
    copy(r2.at[:15], r2.at[:15], p2_s, p2_r, here).wait_recv()
    total = r2[0].astype(F32)
    for s in range(1, NZ):
        total += r2[s].astype(F32)
    diag = total[1] / tokens_all
    diag_t[...] = diag[:, :KM]
    sc[y, z, c] = (total[0] / (diag + damping[0])).astype(BF16)

    for t in range(1, NZ):
        copy(sc.at[y, z, c], sc.at[y, z, c], sz_s, sz_r.at[z // 4], dev(y, (z + t) % NZ, c)).start()
    groups = [(z // 4 + q) % 4 for q in (0, 1, 3, 2)]
    for q, g in enumerate(groups):
        mine = pl.ds(4 * g, 4)
        width = 4 if q else 3
        copy(sc.at[0, :width, 0], sc.at[0, :width, 0], sz_s, sz_r.at[g], here).wait_recv()
        for yy, cc in quad:
            copy(sc.at[y, mine, c], sc.at[y, mine, c], sq_s, sq_r, dev(yy, z, cc)).start()
    own_o.wait()
    copy(bo.at[:7], bo.at[:7], bo_s, bo_r, here).wait_recv()
    copy(sc.at[:, :12], sc.at[:, :12], sq_s, sq_r, here).wait_recv()

    total = jnp.zeros((128, 128), F32)
    for mm in range(NM):
        yy, z0 = mm // 4, 4 * (mm % 4)
        total += jnp.dot(bo[mm], sc[yy, z0:z0 + 4].reshape(128, 128), preferred_element_type=F32)
    bk[m] = total.T[:KM, :].astype(BF16)
    for t in range(1, NM):
        copy(bk.at[m], bk.at[m], bk_s, bk_r, {"dp": d, "mp": (m + t) % NM}).start()
    copy(bk.at[:7], bk.at[:7], bk_s, bk_r, here).wait_recv()
    for mm in range(NM):
        yy, z0 = mm // 4, 4 * (mm % 4)
        b_val = bk[mm].astype(F32)
        for i in range(4):
            dst = 40 * (z0 + i) + 20 * yy
            bf[dst:dst + 20, :] = b_val[20 * i:20 * (i + 1), :]
    back_t = bf[...].T.astype(BF16)
    for cc in range(2):
        for off, piece, width in (
            *((cc * HALF + 256 * q, ga.at[cc, q], 256) for q in range(NC)),
            (cc * HALF + NA, gb.at[cc, 0], NB),
            (cc * HALF + NA + NB, gb.at[cc, 1], NB),
        ):
            rhs = piece[...].reshape(NZ * 40, width)
            up = jnp.dot(back_t, rhs, preferred_element_type=F32)
            update[off:off + width, :] = up.T.astype(BF16)

    @pl.when(far)
    def _():
        copy(bout, bout, sw_s, sw_r, here).wait_send()

    def sent(ref, ssem):
        copy(ref, ref, ssem, sw_r, here).wait_send()

    sent(qa.at[:3], q_s.at[0])
    sent(qb.at[:3], q_s.at[1])
    sent(bo.at[:7], bo_s)
    sent(snd_a.at[:7], xa_s)
    sent(snd_g.at[:7], xg_s)
    sent(gt.at[:15], gt_s)
    sent(act.at[0, :KM], ac_s)
    sent(bk.at[:7], bk_s)
    sent(r1, p1_s)
    sent(p2.at[:15], p2_s)
    sent(sc.at[0, :15, 0], sz_s)
    sent(sc.at[:, :12], sq_s)
    sent(ga.at[0, :, :15], ra_s)
    sent(gb.at[0, 0, :15], rb_s)
    sent(sb.at[0, :15, 0], rs_s)
    sent(gb.at[0, 0], yb_s)
    sent(sb.at[0, :, 0], ys_s)
    sent(ga.at[0], ca_s)
    sent(gb.at[0], cb_s)
    sent(sb.at[:, :, 0], cs_s)


def solution(mesh):
    def on_device(acts, grads, basis_in, basis_out, damping):
        tokens_all = acts.shape[0] * mesh.shape["dp"]
        vmem = pl.BlockSpec(memory_space=pltpu.VMEM)
        dma = pltpu.SemaphoreType.DMA
        v = pltpu.VMEM

        def hbm(array):
            return pltpu.with_memory_space_constraint(array, pltpu.MemorySpace.HBM)

        def body(*refs):
            kernel(tokens_all, *refs)

        update, diag_t = pl.pallas_call(
            body,
            out_shape=(
                jax.ShapeDtypeStruct((3584, 128), BF16),
                jax.ShapeDtypeStruct((16, KM), F32),
            ),
            in_specs=[pl.BlockSpec(memory_space=pltpu.MemorySpace.HBM)] * 4 + [pl.BlockSpec(memory_space=pltpu.SMEM)],
            out_specs=(vmem, vmem),
            scratch_shapes=[
                v(acts.shape, BF16), v(grads.shape, BF16),
                v((NQ, KD, NA), BF16), v((NQ, KD, NB), BF16), v((KM, NA + NB), F32),
                v((2, NC, NZ, 40, 256), BF16), v((2, 2, NZ, 40, NB), BF16),
                v((2, NZ, 2, 128, 128), BF16), v((NM, 128, 128), BF16), v((640, 256), F32),
                v((NM, KM, 256), BF16), v((NM, 256, 128), BF16),
                v((NM, KM, 256), BF16), v((NM, 256, 128), BF16),
                v((2, 128, 256), BF16), v((2, 64, 256), BF16), v((2 * NM, 64, 256), BF16),
                v((2, NZ, 2, 16, 128), BF16), v((NZ, 2, 16, 128), BF16),
                v((NZ, 2, 16, 128), BF16), v((NZ, 2, 16, 128), BF16),
                v((2, NZ, 2, 16, 128), BF16), v((NM, KM, 128), BF16), v((640, 128), F32),
                dma((2,)), dma((2,)), dma, dma((NC, NZ)), dma, dma((NZ,)), dma, dma((NZ,)),
                dma, dma((NZ,)), dma, dma((NZ,)),
                dma, dma, dma, dma, dma, dma((2,)), dma, dma, dma, dma,
                dma, dma, dma, dma, dma, dma,
                dma, dma((4,)), dma, dma,
                dma, dma((4,)), dma, dma, dma, dma, dma((6,)), dma, dma,
            ],
            compiler_params=pltpu.CompilerParams(
                collective_id=0, has_side_effects=True, vmem_limit_bytes=40 * 2**20
            ),
        )(hbm(acts), hbm(grads), hbm(basis_in.T), hbm(basis_out), damping)
        return update, diag_t.T

    placed = (P("dp", "mp"), P("dp", "mp"), P("mp", "dp"), P("dp", "mp"), P())
    return jax.shard_map(
        on_device,
        mesh=mesh,
        in_specs=placed,
        out_specs=(P("mp", "dp"), P("mp", "dp")),
        check_vma=False,
    )
```

time: 1080 us -> 116 us (0.11)
  waiting for transfers between devices: 944 us -> 0 us
  Pallas kernels: 0 us -> 113 us
  blocking collectives: 89.1 us -> 0 us
  matrix products: 15.9 us -> 0 us
  between operations: 15.5 us -> 1.29 us
  local copies, waits for them, and re-layouts: 12.7 us -> 1.52 us
    unnamed x8 -> x0, waiting for transfers between devices: 440 us -> none
    all_gather x5 -> x0, waiting for transfers between devices: 413 us -> none  [the longest x1 128 us: on_device(): lax.all_gather(basis_out, 'dp', axis=0, tiled=True)]
    pallas_call x0 -> x1, Pallas kernels: none -> 113 us  [on_device(): pl.pallas_call(body, out_shape=(jax.ShapeDtypeStruct((3584, 128), BF16),...]
    reduce_scatter x1 -> x0, waiting for transfers between devices: 91.5 us -> none  [on_device(): lax.psum_scatter(lax.dot_general(full_in, acts, (((0,), (1,)), ((), ())),...]
    all_gather x2 -> x0, blocking collectives: 89.1 us -> none  [the longest x1 63.4 us: on_device(): scaled_wide = lax.all_gather(scaled, 'dp', axis=1, tiled=True)]
    dot_general x5 -> x0, matrix products: 15.9 us -> none  [the longest x1 4.67 us: on_device(): update = jnp.dot(full_in, back, preferred_element_type=jnp.float32)]
  transfers between devices with their start and end apart: 7 -> 0, of which waited for: 7 -> 0; matrix products, arithmetic and copies ran while one was open for 2% -> 0% of each run, Pallas kernels for 0% -> 0%
where the time goes in v2:
time: 116 us
  Pallas kernels  113 us (97%)
  local copies, waits for them, and re-layouts  1.52 us (1%)
  between operations  1.29 us (1%)
    pallas_call x1, Pallas kernels, on_device(): pl.pallas_call(body, out_shape=(jax.ShapeDtypeStruct((3584, 128), BF16),...  113 us

profile of v2, /device:TPU:1, one launch (start us, length us, event | category | flops | bytes accessed | tf_op | source)
XLA Modules:
  0.0 116.1 jit_solution(7359333521800340072)
XLA Ops:
  1.3 113.3 %shard_map.68 = (bf16[3584,128]{1,0:T(8,128)(2,1)S(1)}, f32[16,80]{1,0:T(8,128)S(1)}) custom-call(bf16[256,3584]{1,0:T(8,128)(2,1)} %refs_0_.1, bf16[256,1024]{1,0:T(8,128)(2,1)} %refs_1_.1, bf16[10,3584]{1,0:T(8,128)(2,1)} %bitcast.3, bf16[128,128]{1,0:T(8,128)(2,1)} %refs_3_.1, f32[1]{0:T(128)S(6)} %copy.9.refs_4_), custom_call_target="tpu_custom_call" | custom-call | tf_op jit(solution)/shard_map/pallas_call | solution.py:450
  114.5 0.9 copy.10
  115.5 0.6 copy.11

commit v3 on v2

--- a/solution.py
+++ b/solution.py
@@ -17,7 +17,6 @@
 NA = 1024
 NB = 384
 HALF = NA + 2 * NB
-SLAG = 1
 NC = 4
 YLAG = 2
 
@@ -26,8 +25,8 @@
     tokens_all,
     acts_h, grads_h, bin_t, bout, damping,
     update, diag_t,
-    acts, grads,
-    qa, qb, mix, ga, gb, sb, bo, acc,
+    acts, grads, bin_v,
+    qa, qb, mix, ga, gb, sb, bo, bt, acc,
     snd_a, snd_g, rcv_a, rcv_g, act, own_g, gt, part, r1, p2, r2, sc, bk, bf,
     q_s, q_r, ra_s, ra_r, rb_s, rb_r, yb_s, yb_r, rs_s, rs_r, ys_s, ys_r,
     ca_s, ca_r, cb_s, cb_r, cs_s, cs_r, sw_s, sw_r, bo_s, bo_r,
@@ -83,34 +82,37 @@
 
     a_off = pl.multiple_of(c * HALF, 128)
     b_off = pl.multiple_of(c * HALF + NA + y * NB, 128)
-    own_a = pltpu.make_async_copy(bin_t.at[:, pl.ds(a_off, NA)], qa.at[me_q], in_s.at[0])
-    own_b = pltpu.make_async_copy(bin_t.at[:, pl.ds(b_off, NB)], qb.at[me_q], in_s.at[1])
+    get_b = pltpu.make_async_copy(bin_t, bin_v, in_s.at[0])
     own_o = pltpu.make_async_copy(bout, bo.at[m], in_s.at[2])
-    own_s = pltpu.make_async_copy(bout, sb.at[y, z, c], in_s.at[3])
     get_g = pltpu.make_async_copy(grads_h, grads, in_s.at[4])
     get_a = pltpu.make_async_copy(acts_h, acts, in_s.at[5])
-    own_a.start()
-    own_b.start()
     own_o.start()
+    get_b.start()
+
+    get_g.start()
+    get_a.start()
+    own_o.wait()
+    bt[...] = bo[m].astype(F32).T.astype(BF16)
+    get_b.wait()
+    qa[me_q] = bin_v[:, pl.ds(a_off, NA)]
+    qb[me_q] = bin_v[:, pl.ds(b_off, NB)]
 
     @pl.when(jnp.logical_not(far))
     def _():
-        own_s.start()
-
-    get_g.start()
-    get_a.start()
+        sb[y, z, c] = bt[...]
+
     pl.semaphore_wait(barrier, NZ - 1 + 3 + 2 * (NM - 1) + far.astype(jnp.int32))
 
     @pl.when(far)
     def _():
-        copy(bout, sb.at[swap_d // 32, (swap_d // 2) % 16, swap_d % 2], sw_s, sw_r,
+        copy(bt, sb.at[swap_d // 32, (swap_d // 2) % 16, swap_d % 2], sw_s, sw_r,
              {"dp": swap_d, "mp": swap_a}).start()
 
     for yy, cc in quad:
         a_to = pl.multiple_of(cc * HALF, 128)
         b_to = pl.multiple_of(cc * HALF + NA + yy * NB, 128)
-        copy(bin_t.at[:, pl.ds(a_to, NA)], qa.at[me_q], q_s.at[0], q_r.at[0], dev(yy, z, cc)).start()
-        copy(bin_t.at[:, pl.ds(b_to, NB)], qb.at[me_q], q_s.at[1], q_r.at[1], dev(yy, z, cc)).start()
+        copy(bin_v.at[:, pl.ds(a_to, NA)], qa.at[me_q], q_s.at[0], q_r.at[0], dev(yy, z, cc)).start()
+        copy(bin_v.at[:, pl.ds(b_to, NB)], qb.at[me_q], q_s.at[1], q_r.at[1], dev(yy, z, cc)).start()
     for t in range(1, NM):
         copy(bout, bo.at[m], bo_s, bo_r, {"dp": d, "mp": (m + t) % NM}).start()
 
@@ -166,8 +168,6 @@
         copy(sb.at[oy, zz, c], sb.at[oy, zz, c], ys_s, ys_r.at[zz], here).wait_recv()
         core_s(oy, zz)
 
-    own_a.wait()
-    own_b.wait()
     copy(qa.at[:3], qa.at[:3], q_s.at[0], q_r.at[0], here).wait_recv()
     copy(qb.at[:3], qb.at[:3], q_s.at[1], q_r.at[1], here).wait_recv()
     for s in range(NQ):
@@ -185,26 +185,27 @@
     ring_b(z, left)
     side_b(z)
 
-    def hop(t, got, ring, side):
+    @pl.when(far)
+    def _():
+        copy(sb.at[y, z, c], sb.at[y, z, c], sw_s, sw_r, here).wait_recv()
+
+    ring_s(z, right)
+    ring_s(z, left)
+    side_s(z)
+
+    def hop(t, got, ring, side, last):
         zr = (z - t + NZ) % NZ
         zl = (z + t) % NZ
-        got(zr)
-
-        @pl.when(t < 8)
-        def _():
-            ring(zr, right)
-
-        side(zr)
-
-        @pl.when(t < 8)
-        def _():
-            got(zl)
-
-            @pl.when(t < 7)
+        for zz, device, reach in ((zr, right, 8 if last == 0 else 7), (zl, left, 8 if last == 1 else 7)):
+            @pl.when(t <= reach)
             def _():
-                ring(zl, left)
-
-            side(zl)
+                got(zz)
+
+                @pl.when(t < reach)
+                def _():
+                    ring(zz, device)
+
+                side(zz)
 
     def side_hop(t, got):
         got((z - t + NZ) % NZ)
@@ -217,44 +218,32 @@
         @pl.when(s <= 8)
         def _():
             for q in range(NC):
-                hop(s, got_a(q), ring_a(q), core_a(q))
-            hop(s, got_b, ring_b, side_b)
-
-        @pl.when(s == SLAG)
-        def _():
-            @pl.when(far)
-            def _():
-                copy(sb.at[y, z, c], sb.at[y, z, c], sw_s, sw_r, here).wait_recv()
-
-            @pl.when(jnp.logical_not(far))
-            def _():
-                own_s.wait()
-
-            ring_s(z, right)
-            ring_s(z, left)
-            side_s(z)
-
-        @pl.when((s > SLAG) & (s <= SLAG + 8))
-        def _():
-            hop(s - SLAG, got_s, ring_s, side_s)
-
-        @pl.when((s >= YLAG) & (s <= YLAG + 8))
+                hop(s, got_a(q), ring_a(q), core_a(q), q % 2)
+            hop(s, got_b, ring_b, side_b, 0)
+            hop(s, got_s, ring_s, side_s, 1)
+
+        @pl.when(s >= YLAG)
         def _():
             side_hop(s - YLAG, got_yb)
-
-        @pl.when(s >= SLAG + YLAG)
-        def _():
-            side_hop(s - SLAG - YLAG, got_ys)
+            side_hop(s - YLAG, got_ys)
 
         return 0
 
     def grad_part(col):
         copy(sb.at[col, :, oc], sb.at[col, :, oc], cs_s, cs_r.at[col], here).wait_recv()
+        prod = None
+        for zz in range(4):
+            lhs = jnp.concatenate(
+                [jnp.concatenate([sb[col, 4 * b + zz, cc] for b in range(4)], axis=0) for cc in range(2)], axis=1
+            )
+            term = lax.dot_general(
+                lhs, grads[:, 256 * zz:256 * (zz + 1)], (((1,), (1,)), ((), ())), preferred_element_type=F32
+            )
+            prod = term if prod is None else prod + term
+        for b in range(4):
+            snd_g[4 * col + b] = prod[128 * b:128 * (b + 1), :].astype(BF16)
         for k in (2, 1, 3, 0):
-            z0 = (m % 4 + k) % 4
-            to = 4 * col + z0
-            block = sb[col, pl.ds(4 * z0, 4)].reshape(1024, 128)
-            snd_g[to] = jnp.dot(grads[...], block, preferred_element_type=F32).astype(BF16)
+            to = 4 * col + (m % 4 + k) % 4
 
             @pl.when(to != m)
             def _():
@@ -298,19 +287,17 @@
 
     lax.fori_loop(1, 9, step, 0)
     act_first()
-    lax.fori_loop(9, 9 + SLAG, step, 0)
+    lax.fori_loop(9, 9 + YLAG, step, 0)
     get_g.wait()
-    grad_part(y)
-    lax.fori_loop(9 + SLAG, 9 + YLAG, step, 0)
+    grad_part(1 - m // 4)
+    grad_part(m // 4)
     act_rest()
-    lax.fori_loop(9 + YLAG, 9 + SLAG + YLAG, step, 0)
-    grad_part(oy)
 
     copy(rcv_g.at[:7], rcv_g.at[:7], xg_s, xg_r, here).wait_recv()
     total = rcv_g[0].astype(F32)
     for s in range(1, NM):
         total += rcv_g[s].astype(F32)
-    g_t = total.T.astype(BF16)
+    g_t = total.astype(BF16)
     for i in range(8):
         own_g[i % 2, 16 * (i // 2):16 * (i // 2 + 1), :] = g_t[16 * i:16 * (i + 1), :]
     mine_g = c * NM + m
@@ -376,7 +363,6 @@
         copy(sc.at[0, :width, 0], sc.at[0, :width, 0], sz_s, sz_r.at[g], here).wait_recv()
         for yy, cc in quad:
             copy(sc.at[y, mine, c], sc.at[y, mine, c], sq_s, sq_r, dev(yy, z, cc)).start()
-    own_o.wait()
     copy(bo.at[:7], bo.at[:7], bo_s, bo_r, here).wait_recv()
     copy(sc.at[:, :12], sc.at[:, :12], sq_s, sq_r, here).wait_recv()
 
@@ -407,7 +393,7 @@
 
     @pl.when(far)
     def _():
-        copy(bout, bout, sw_s, sw_r, here).wait_send()
+        copy(bt, bt, sw_s, sw_r, here).wait_send()
 
     def sent(ref, ssem):
         copy(ref, ref, ssem, sw_r, here).wait_send()
@@ -456,12 +442,12 @@
             in_specs=[pl.BlockSpec(memory_space=pltpu.MemorySpace.HBM)] * 4 + [pl.BlockSpec(memory_space=pltpu.SMEM)],
             out_specs=(vmem, vmem),
             scratch_shapes=[
-                v(acts.shape, BF16), v(grads.shape, BF16),
+                v(acts.shape, BF16), v(grads.shape, BF16), v((KD, acts.shape[1]), BF16),
                 v((NQ, KD, NA), BF16), v((NQ, KD, NB), BF16), v((KM, NA + NB), F32),
                 v((2, NC, NZ, 40, 256), BF16), v((2, 2, NZ, 40, NB), BF16),
-                v((2, NZ, 2, 128, 128), BF16), v((NM, 128, 128), BF16), v((640, 256), F32),
-                v((NM, KM, 256), BF16), v((NM, 256, 128), BF16),
-                v((NM, KM, 256), BF16), v((NM, 256, 128), BF16),
+                v((2, NZ, 2, 128, 128), BF16), v((NM, 128, 128), BF16), v((128, 128), BF16), v((640, 256), F32),
+                v((NM, KM, 256), BF16), v((NM, 128, 256), BF16),
+                v((NM, KM, 256), BF16), v((NM, 128, 256), BF16),
                 v((2, 128, 256), BF16), v((2, 64, 256), BF16), v((2 * NM, 64, 256), BF16),
                 v((2, NZ, 2, 16, 128), BF16), v((NZ, 2, 16, 128), BF16),
                 v((NZ, 2, 16, 128), BF16), v((NZ, 2, 16, 128), BF16),

time: 116 us -> 109 us (0.940)
  Pallas kernels: 113 us -> 106 us
    pallas_call x1, Pallas kernels: 113 us -> 106 us  [on_device(): pl.pallas_call(body, out_shape=(jax.ShapeDtypeStruct((3584, 128), BF16),...]
where the time goes in v3:
time: 109 us
  Pallas kernels  106 us (97%)
  local copies, waits for them, and re-layouts  1.52 us (1%)
  between operations  1.29 us (1%)
    pallas_call x1, Pallas kernels, on_device(): pl.pallas_call(body, out_shape=(jax.ShapeDtypeStruct((3584, 128), BF16),...  106 us

profile of v3, /device:TPU:1, one launch (start us, length us, event | category | flops | bytes accessed | tf_op | source)
XLA Modules:
  0.0 108.8 jit_solution(5074576932060159737)
XLA Ops:
  1.3 106.0 %shard_map.68 = (bf16[3584,128]{1,0:T(8,128)(2,1)S(1)}, f32[16,80]{1,0:T(8,128)S(1)}) custom-call(bf16[256,3584]{1,0:T(8,128)(2,1)} %refs_0_.1, bf16[256,1024]{1,0:T(8,128)(2,1)} %refs_1_.1, bf16[10,3584]{1,0:T(8,128)(2,1)} %bitcast.3, bf16[128,128]{1,0:T(8,128)(2,1)} %refs_3_.1, f32[1]{0:T(128)S(6)} %copy.9.refs_4_), custom_call_target="tpu_custom_call" | custom-call | tf_op jit(solution)/shard_map/pallas_call | solution.py:436
  107.3 0.9 copy.10
  108.2 0.6 copy.11

commit v4 on v3

--- a/solution.py
+++ b/solution.py
@@ -319,18 +319,31 @@
 
     nt = (((1,), (1,)), ((), ()))
     groups = [(z // 4 + q) % 4 for q in (2, 1, 3, 0)]
+    squares = [(act[cc].astype(F32) ** 2).astype(BF16) for cc in range(2)]
+
+    def rows(*pieces):
+        return jnp.concatenate(
+            [jnp.zeros((q, 256), BF16) if isinstance(q, int) else q for q in pieces], axis=0
+        )
+
     for half in (oy, y):
-        rot = jnp.zeros((256, 128), F32)
-        sq = jnp.zeros((256, 128), F32)
+        full = jnp.zeros((256, 128), F32)
+        rest = jnp.zeros((128, 128), F32)
         for cc in range(2):
-            a_val = act[cc]
+            a_sq = squares[cc]
             g_val = gt[pl.ds(cc * NM + 4 * half, 4)].reshape(256, 256)
-            rot += lax.dot_general(g_val, a_val, nt, preferred_element_type=F32)
-            a_sq = (a_val.astype(F32) ** 2).astype(BF16)
             g_sq = (g_val.astype(F32) ** 2).astype(BF16)
-            sq += lax.dot_general(g_sq, a_sq, nt, preferred_element_type=F32)
-        part[half, :, 0] = rot.astype(BF16).reshape(NZ, 16, 128)
-        part[half, :, 1] = sq.astype(BF16).reshape(NZ, 16, 128)
+            parts = g_sq.reshape(NZ, 2, 8, 256)
+            full += lax.dot_general(g_val, act[cc], nt, preferred_element_type=F32)
+            full += lax.dot_general(g_sq, rows(KM, a_sq[:48]), nt, preferred_element_type=F32)
+            rest += lax.dot_general(
+                parts[:, 0].reshape(128, 256), rows(a_sq[48:KM], 96), nt, preferred_element_type=F32
+            )
+            rest += lax.dot_general(
+                parts[:, 1].reshape(128, 256), rows(32, a_sq[48:KM], 64), nt, preferred_element_type=F32
+            )
+        part[half, :, :16] = full.astype(BF16).reshape(NZ, 16, 128)
+        part[half, :, 16:] = rest.astype(BF16).reshape(NZ, 8, 128)
         if half is oy:
             for q, g in enumerate(groups):
                 mine = pl.ds(4 * g, 4)
@@ -350,9 +363,11 @@
     total = r2[0].astype(F32)
     for s in range(1, NZ):
         total += r2[s].astype(F32)
-    diag = total[1] / tokens_all
-    diag_t[...] = diag[:, :KM]
-    sc[y, z, c] = (total[0] / (diag + damping[0])).astype(BF16)
+    last = jnp.concatenate([total[16:, :32], total[16:, 32:64]], axis=0)
+    diag = jnp.concatenate([total[:16, KM:], last], axis=1) / tokens_all
+    diag_t[...] = diag
+    scaled = total[:16, :KM] / (diag + damping[0])
+    sc[y, z, c] = jnp.concatenate([scaled, jnp.zeros((16, 128 - KM), F32)], axis=1).astype(BF16)
 
     for t in range(1, NZ):
         copy(sc.at[y, z, c], sc.at[y, z, c], sz_s, sz_r.at[z // 4], dev(y, (z + t) % NZ, c)).start()
@@ -449,8 +464,8 @@
                 v((NM, KM, 256), BF16), v((NM, 128, 256), BF16),
                 v((NM, KM, 256), BF16), v((NM, 128, 256), BF16),
                 v((2, 128, 256), BF16), v((2, 64, 256), BF16), v((2 * NM, 64, 256), BF16),
-                v((2, NZ, 2, 16, 128), BF16), v((NZ, 2, 16, 128), BF16),
-                v((NZ, 2, 16, 128), BF16), v((NZ, 2, 16, 128), BF16),
+                v((2, NZ, 24, 128), BF16), v((NZ, 24, 128), BF16),
+                v((NZ, 24, 128), BF16), v((NZ, 24, 128), BF16),
                 v((2, NZ, 2, 16, 128), BF16), v((NM, KM, 128), BF16), v((640, 128), F32),
                 dma((2,)), dma((2,)), dma, dma((NC, NZ)), dma, dma((NZ,)), dma, dma((NZ,)),
                 dma, dma((NZ,)), dma, dma((NZ,)),

time: 109 us -> 108 us (level)
  no operation moved by 1% of the time
where the time goes in v4:
time: 108 us
  Pallas kernels  105 us (97%)
  local copies, waits for them, and re-layouts  1.52 us (1%)
  between operations  1.29 us (1%)
    pallas_call x1, Pallas kernels, on_device(): pl.pallas_call(body, out_shape=(jax.ShapeDtypeStruct((3584, 128), BF16),...  105 us

profile of v4, /device:TPU:1, one launch (start us, length us, event | category | flops | bytes accessed | tf_op | source)
XLA Modules:
  0.0 108.2 jit_solution(5042428574430018853)
XLA Ops:
  1.3 105.4 %shard_map.68 = (bf16[3584,128]{1,0:T(8,128)(2,1)S(1)}, f32[16,80]{1,0:T(8,128)S(1)}) custom-call(bf16[256,3584]{1,0:T(8,128)(2,1)} %refs_0_.1, bf16[256,1024]{1,0:T(8,128)(2,1)} %refs_1_.1, bf16[10,3584]{1,0:T(8,128)(2,1)} %bitcast.3, bf16[128,128]{1,0:T(8,128)(2,1)} %refs_3_.1, f32[1]{0:T(128)S(6)} %copy.9.refs_4_), custom_call_target="tpu_custom_call" | custom-call | tf_op jit(solution)/shard_map/pallas_call | solution.py:451
  106.7 0.9 copy.10
  107.6 0.6 copy.11

commit v5 on v4

--- a/solution.py
+++ b/solution.py
@@ -58,6 +58,10 @@
     core = dev(y, z, oc)
     yside = dev(oy, z, c)
     quad = [(y, oc), (oy, c), (oy, oc)]
+    peers = [
+        4 * ((m // 4 + a) % 2) + (m % 4 + b) % 4
+        for a, b in ((1, 2), (1, 1), (1, 3), (1, 0), (0, 2), (0, 1), (0, 3))
+    ]
     swap_a = d // 8
     swap_d = 8 * m + d % 8
     far = swap_a != m
@@ -113,8 +117,8 @@
         b_to = pl.multiple_of(cc * HALF + NA + yy * NB, 128)
         copy(bin_v.at[:, pl.ds(a_to, NA)], qa.at[me_q], q_s.at[0], q_r.at[0], dev(yy, z, cc)).start()
         copy(bin_v.at[:, pl.ds(b_to, NB)], qb.at[me_q], q_s.at[1], q_r.at[1], dev(yy, z, cc)).start()
-    for t in range(1, NM):
-        copy(bout, bo.at[m], bo_s, bo_r, {"dp": d, "mp": (m + t) % NM}).start()
+    for to in peers:
+        copy(bout, bo.at[m], bo_s, bo_r, {"dp": d, "mp": to}).start()
 
     def ring_a(q):
         def send(zz, device):
@@ -279,8 +283,7 @@
                 src = 40 * (z0 + i) + 20 * yy
                 mix[20 * i:20 * (i + 1), :256] = acc[src:src + 20, :]
             snd_a[mm] = mix[:KM, :256].astype(BF16)
-        for t in range(1, NM):
-            to = (m + t) % NM
+        for to in peers:
             copy(snd_a.at[to], rcv_a.at[m], xa_s, xa_r, {"dp": d, "mp": to}).start()
         rcv_a[m] = snd_a[m]
 
@@ -301,8 +304,7 @@
     for i in range(8):
         own_g[i % 2, 16 * (i // 2):16 * (i // 2 + 1), :] = g_t[16 * i:16 * (i + 1), :]
     mine_g = c * NM + m
-    for t in range(1, NM):
-        to = (m + t) % NM
+    for to in peers:
         copy(own_g.at[c], gt.at[mine_g], gt_s, gt_r, {"dp": d, "mp": to}).start()
         copy(own_g.at[oc], gt.at[mine_g], gt_s, gt_r, {"dp": d_other, "mp": to}).start()
     copy(own_g.at[oc], gt.at[mine_g], gt_s, gt_r, core).start()
@@ -369,12 +371,12 @@
     scaled = total[:16, :KM] / (diag + damping[0])
     sc[y, z, c] = jnp.concatenate([scaled, jnp.zeros((16, 128 - KM), F32)], axis=1).astype(BF16)
 
-    for t in range(1, NZ):
+    for t in (8, 7, 9, 6, 10, 5, 11, 4, 12, 3, 13, 2, 14, 1, 15):
         copy(sc.at[y, z, c], sc.at[y, z, c], sz_s, sz_r.at[z // 4], dev(y, (z + t) % NZ, c)).start()
-    groups = [(z // 4 + q) % 4 for q in (0, 1, 3, 2)]
+    groups = [(z // 4 + q) % 4 for q in (2, 1, 3, 0)]
     for q, g in enumerate(groups):
         mine = pl.ds(4 * g, 4)
-        width = 4 if q else 3
+        width = 4 if q < 3 else 3
         copy(sc.at[0, :width, 0], sc.at[0, :width, 0], sz_s, sz_r.at[g], here).wait_recv()
         for yy, cc in quad:
             copy(sc.at[y, mine, c], sc.at[y, mine, c], sq_s, sq_r, dev(yy, z, cc)).start()
@@ -386,8 +388,8 @@
         yy, z0 = mm // 4, 4 * (mm % 4)
         total += jnp.dot(bo[mm], sc[yy, z0:z0 + 4].reshape(128, 128), preferred_element_type=F32)
     bk[m] = total.T[:KM, :].astype(BF16)
-    for t in range(1, NM):
-        copy(bk.at[m], bk.at[m], bk_s, bk_r, {"dp": d, "mp": (m + t) % NM}).start()
+    for to in peers:
+        copy(bk.at[m], bk.at[m], bk_s, bk_r, {"dp": d, "mp": to}).start()
     copy(bk.at[:7], bk.at[:7], bk_s, bk_r, here).wait_recv()
     for mm in range(NM):
         yy, z0 = mm // 4, 4 * (mm % 4)

time: 108 us -> 109 us (level); the launches traced: 108 us -> 108 us
  no operation moved by 1% of the time
where the time goes in v5:
time: 109 us; the launch traced here: 108 us
  Pallas kernels  105 us (96%)
  local copies, waits for them, and re-layouts  1.52 us (1%)
  between operations  1.29 us (1%)
    pallas_call x1, Pallas kernels, on_device(): pl.pallas_call(body, out_shape=(jax.ShapeDtypeStruct((3584, 128), BF16),...  105 us

profile of v5, /device:TPU:1, one launch (start us, length us, event | category | flops | bytes accessed | tf_op | source)
XLA Modules:
  0.0 107.9 jit_solution(2120522463419709378)
XLA Ops:
  1.3 105.1 %shard_map.68 = (bf16[3584,128]{1,0:T(8,128)(2,1)S(1)}, f32[16,80]{1,0:T(8,128)S(1)}) custom-call(bf16[256,3584]{1,0:T(8,128)(2,1)} %refs_0_.1, bf16[256,1024]{1,0:T(8,128)(2,1)} %refs_1_.1, bf16[10,3584]{1,0:T(8,128)(2,1)} %bitcast.3, bf16[128,128]{1,0:T(8,128)(2,1)} %refs_3_.1, f32[1]{0:T(128)S(6)} %copy.9.refs_4_), custom_call_target="tpu_custom_call" | custom-call | tf_op jit(solution)/shard_map/pallas_call | solution.py:453
  106.4 0.9 copy.10
  107.3 0.6 copy.11
